TPU v7x, 32 devices: a whole 2x2x4 slice. The times are simulated.
32 devices in a mesh: shard: 2 (over y), tensor: 4 (over x, core), section: 4 (over z).
Axes of the slice: x: 2, y: 2, z: 4, core: 2. Of those that a mesh axis runs over, the one named last changes fastest.
Arguments:
- grad_parts: float32 [2, 4, 4, 1152, 1024], P('shard', 'tensor', 'section'), may hold values from -1 to 1
- master: float32 [1152, 16, 1024], P(('tensor', 'section'), 'shard'), may hold values from -0.1875 to 0.1875
- owner_map: int32 [4, 4], replicated, may hold values from 0 to 1, as said below
- left_factor: float32 [16, 1152, 1152], P('shard', ('tensor', 'section')), may hold values from -1.2 to 11.2, as said below
- right_factor: float32 [16, 1024, 1024], P('shard', ('tensor', 'section')), may hold values from -1.2 to 11.2, as said below
- left_basis: float32 [16, 1152, 1152], P('shard', ('tensor', 'section')), may hold values from -0.1875 to 0.1875
- right_basis: float32 [16, 1024, 1024], P('shard', None, ('tensor', 'section')), may hold values from -0.1875 to 0.1875
- moment_one: float32 [16, 1152, 1024], P('shard', ('tensor', 'section')), may hold values from -3 to 3
- moment_two: float32 [16, 1152, 1024], P('shard', ('tensor', 'section')), may hold values from 0.01 to 0.5
Outputs:
- new_master: float32 [1152, 16, 1024], P(('tensor', 'section'), 'shard')
- update_dir: float32 [1152, 16, 1024], P(('tensor', 'section'), 'shard')
- new_left: float32 [16, 1152, 1152], P('shard', ('tensor', 'section'))
- new_right: float32 [16, 1024, 1024], P('shard', ('tensor', 'section'))
- new_moment_one: float32 [16, 1152, 1024], P('shard', ('tensor', 'section'))
- new_moment_two: float32 [16, 1152, 1024], P('shard', ('tensor', 'section'))
Inputs may be any that keep to these rules, and one draw needn't show every extreme that they name: `owner_map`: each shard index owns exactly 8 matrices. `left_factor`: symmetric in its last two dimensions. `right_factor`: symmetric in its last two dimensions.
All inputs are finite; a program needn't handle non-finite values.
Results may differ from a plain program's by a relative error of at most 0.0003.
Values sent between devices are 32-bit elements; how exact they have to be, the bound alone decides.
A program may use at most 448 MiB of HBM per device.

v0:
```python
import jax
import jax.numpy as jnp
from jax import lax
from jax.sharding import PartitionSpec as P

beta_one = 0.95
beta_two = 0.95
epsilon = 1e-08
learn_rate = 0.01
decay_weight = 0.1
step_count = 10


def slot_table(owner_map, shards):
    owners_flat = owner_map.reshape(-1)
    matrices = owners_flat.shape[0]
    per_owner = matrices // shards
    member = (owners_flat[:, None] == jnp.arange(shards, dtype=jnp.int32)[None, :]).astype(
        jnp.int32
    )
    before = jnp.cumsum(member, axis=0) - member
    rank_in = jnp.sum(before * member, axis=1)
    slot_of = owners_flat * per_owner + rank_in
    places = (slot_of[:, None] == jnp.arange(matrices, dtype=jnp.int32)[None, :]).astype(jnp.int32)
    source = jnp.sum(places * jnp.arange(matrices, dtype=jnp.int32)[:, None], axis=0)
    return (slot_of, source)


def local(
    grad_parts,
    master,
    owner_map,
    left_factor,
    right_factor,
    left_basis,
    right_basis,
    moment_one,
    moment_two,
):
    exact_mode = lax.Precision.HIGHEST
    shards = lax.axis_size("shard")
    members = lax.axis_size(("tensor", "section"))
    position = lax.axis_index(("tensor", "section"))
    slot_of, source = slot_table(owner_map, shards)
    height = left_basis.shape[2]
    width = right_basis.shape[1]
    row_block = height // members
    col_block = width // members
    local_part = grad_parts[0, 0, 0]
    row_piece = lax.psum_scatter(local_part, "shard", scatter_dimension=0, tiled=True)
    stacked = lax.all_gather(row_piece[None], ("tensor", "section"), axis=0, tiled=True)
    ordered = jnp.take(stacked, source, axis=0)
    full_grad = lax.all_to_all(ordered, "shard", split_axis=0, concat_axis=1, tiled=True)
    full_right = lax.all_gather(right_basis, ("tensor", "section"), axis=2, tiled=True)
    grad_band = lax.dynamic_slice_in_dim(full_grad, position * row_block, row_block, 1)
    grad_slab = lax.dynamic_slice_in_dim(full_grad, position * col_block, col_block, 2)
    new_left = beta_two * left_factor + (1.0 - beta_two) * jnp.einsum(
        "orn,ofn->orf", grad_band, full_grad, precision=exact_mode
    )
    new_right = beta_two * right_factor + (1.0 - beta_two) * jnp.einsum(
        "ofc,ofn->ocn", grad_slab, full_grad, precision=exact_mode
    )
    turned = jnp.einsum("orf,ofn->orn", left_basis, full_grad, precision=exact_mode)
    rotated = jnp.einsum("orn,onk->ork", turned, full_right, precision=exact_mode)
    new_moment_one = beta_one * moment_one + (1.0 - beta_one) * rotated
    new_moment_two = beta_two * moment_two + (1.0 - beta_two) * rotated * rotated
    first_fix = 1.0 - beta_one**step_count
    second_fix = 1.0 - beta_two**step_count
    scaled = new_moment_one / first_fix / (jnp.sqrt(new_moment_two / second_fix) + epsilon)
    pulled = jnp.einsum("orn,okn->ork", scaled, full_right, precision=exact_mode)
    update_dir = lax.psum_scatter(
        jnp.einsum("orf,ork->fok", left_basis, pulled, precision=exact_mode),
        ("tensor", "section"),
        scatter_dimension=0,
        tiled=True,
    )
    new_master = master - learn_rate * (update_dir + decay_weight * master)
    return (new_master, update_dir, new_left, new_right, new_moment_one, new_moment_two)


def solution(mesh):
    placed = (
        P("shard", "tensor", "section", None, None),
        P(("tensor", "section"), "shard", None),
        P(),
        P("shard", ("tensor", "section"), None),
        P("shard", ("tensor", "section"), None),
        P("shard", ("tensor", "section"), None),
        P("shard", None, ("tensor", "section")),
        P("shard", ("tensor", "section"), None),
        P("shard", ("tensor", "section"), None),
    )
    return jax.shard_map(
        local,
        mesh=mesh,
        in_specs=placed,
        out_specs=(
            P(("tensor", "section"), "shard", None),
            P(("tensor", "section"), "shard", None),
            P("shard", ("tensor", "section"), None),
            P("shard", ("tensor", "section"), None),
            P("shard", ("tensor", "section"), None),
            P("shard", ("tensor", "section"), None),
        ),
        check_vma=False,
    )
```

profile of v0, /device:TPU:0, one launch (start us, length us, event | category | flops | bytes accessed | tf_op | source)
XLA Modules:
  0.0 1349.7 jit_solution(5164771268926579444)
XLA Ops:
  7.2 0.0 copy-start
  7.2 0.0 reduce-scatter.3.cloned.1.call-start
  7.2 0.7 reduce-scatter.3.cloned.1.call-update
  7.9 0.0 copy-start.2
  7.9 0.0 all-gather.6.cloned.1.call-start
  8.0 65.1 %reduce-scatter.3.cloned.1.call-done = f32[576,1024]{1,0:T(8,128)} async-done(((f32[1152,1024]{1,0:T(8,128)}), f32[576,1024]{1,0:T(8,128)}) %reduce-scatter.3.cloned.1.call-update) | async-done | bytes 2359312 | tf_op jit(solution)/shard_map/reduce_scatter | solution.py:50
  73.0 0.0 all-gather.6.cloned.1.call-update
  73.1 0.0 all-gather.4.cloned.1.call-start
  73.1 0.7 all-gather.4.cloned.1.call-update
  73.8 0.0 reduce-scatter.5.cloned.1.call-start
  73.8 0.0 copy-done.2
  73.9 0.1 reshape.42
  73.9 0.1 fusion.15
  74.1 0.2 select_reduce_fusion.1
  74.2 0.1 select_reduce_fusion
  74.4 199.3 %all-gather.6.cloned.1.call-done = f32[9216,1024]{1,0:T(8,128)} async-done(((f32[576,1024]{1,0:T(8,128)}), f32[9216,1024]{1,0:T(8,128)}) %all-gather.6.cloned.1.call-update) | async-done | bytes 37748752 | tf_op jit(solution)/shard_map/all_gather | solution.py:51
  273.7 26.5 %gather_fusion = f32[16,576,1024]{2,1,0:T(8,128)} fusion(f32[16,576,1024]{2,1,0:T(8,128)} %bitcast.25, s32[1024]{0:T(1024)S(1)} %pad_clamp_fusion), kind=kCustom, calls=%fused_computation | custom fusion | bytes 75497536 | tf_op jit(solution)/shard_map/jit(_take)/gather | solution.py:52
  300.2 29.8 %broadcast_select_fusion = f32[16,576,1024]{2,1,0:T(8,128)} fusion(f32[16,576,1024]{2,1,0:T(8,128)} %gather_fusion, pred[16]{0:T(512)(128)(4,1)S(1)} %compare_and_fusion), kind=kLoop, calls=%fused_computation.2 | loop fusion | flops 9437184 | bytes 75497488 | tf_op jit(solution)/shard_map/jit(_take)/select_n | solution.py:52
  330.0 443.8 %all_to_all.18 = f32[16,576,1024]{2,1,0:T(8,128)} all-to-all(f32[16,576,1024]{2,1,0:T(8,128)} %broadcast_select_fusion), channel_id=1, replica_groups=mesh['shard'=2,'tensor'=4,'section'=4] {'shard'}, dimensions={0} | all-to-all | bytes 75497472 | tf_op jit(solution)/shard_map/all_to_all | solution.py:53
  773.9 28.0 %copy.29 = f32[8,2,576,1024]{3,2,1,0:T(8,128)} copy(f32[8,2,576,1024]{3,2,0,1:T(8,128)} %bitcast.24) | data formatting | bytes 75497472 | tf_op jit(solution)/shard_map/all_to_all | solution.py:53
  801.8 0.0 copy-done
  801.8 31.9 %fusion.21 = f32[8,1024,72]{1,2,0:T(8,128)} fusion(f32[8,1152,1024]{2,1,0:T(8,128)} %bitcast.21, f32[8,72,1152]{2,1,0:T(8,128)S(1)} %copy-done), kind=kOutput, calls=%fused_computation.36 | convolution fusion | flops 8153726976 | bytes 42762240 | tf_op jit(solution)/shard_map/orf,ofn->orn/dot_general | solution.py:63
  833.8 38.4 %multiply_add_fusion = (f32[8,72,1024]{2,1,0:T(8,128)}, f32[8,72,1024]{2,1,0:T(8,128)}) fusion(f32[8,72,1024]{2,1,0:T(8,128)} %param.16, f32[8,72,1024]{2,1,0:T(8,128)} %param.17, f32[8,1024,72]{1,2,0:T(8,128)} %fusion.21, f32[8,1024,1024]{1,2,0:T(8,128)} %all-gather.4.cloned.1.call-done), kind=kOutput, calls=%fused_computation.8 | convolution fusion | flops 7251296256 | bytes 45350912 | tf_op jit(solution)/shard_map/orn,onk->ork/dot_general | solution.py:64
  872.1 26.8 %fusion.5 = f32[8,72,1024]{2,1,0:T(8,128)} fusion(f32[8,1024,1024]{1,2,0:T(8,128)} %all-gather.4.cloned.1.call-done, f32[8,72,1024]{2,1,0:T(8,128)} %get-tuple-element.19, f32[8,72,1024]{2,1,0:T(8,128)} %get-tuple-element.18), kind=kOutput, calls=%fused_computation.12 | convolution fusion | flops 7250116608 | bytes 40632320 | tf_op jit(solution)/shard_map/orn,okn->ork/dot_general | solution.py:70
  898.9 34.9 %convolution_bitcast_fusion = f32[1152,8,1024]{0,2,1:T(8,128)} fusion(f32[8,72,1024]{2,1,0:T(8,128)} %fusion.5, f32[8,72,1152]{2,1,0:T(8,128)S(1)} %copy-done), kind=kOutput, calls=%fused_computation.1 | convolution fusion | flops 8153726976 | bytes 42762240 | tf_op jit(solution)/shard_map/orf,ork->fok/dot_general | solution.py:72
  933.8 37.2 %copy.30 = f32[1152,8,1024]{2,1,0:T(8,128)} copy(f32[1152,8,1024]{0,2,1:T(8,128)} %convolution_bitcast_fusion) | data formatting | bytes 75497472 | tf_op jit(solution)/shard_map/orf,ork->fok/transpose | solution.py:72
  971.0 0.0 reduce-scatter.5.cloned.1.call-update
  971.1 0.0 copy-start.1
  971.1 43.9 %multiply_add_fusion.1 = f32[8,64,1024]{2,1,0:T(8,128)} fusion(f32[8,64,1024]{2,1,0:T(8,128)} %param.13, f32[8,1152,1024]{2,1,0:T(8,128)} %bitcast.22, s32[]{:T(128)S(6)} %select_n.30), kind=kOutput, calls=%fused_computation.18 | convolution fusion | flops 7249330176 | bytes 46661636 | tf_op jit(solution)/shard_map/ofc,ofn->ocn/dot_general | solution.py:60
  1014.9 42.9 %fusion.2 = f32[8,72,1152]{2,1,0:T(8,128)} fusion(f32[8,1152,1024]{2,1,0:T(8,128)} %bitcast.23, f32[8,72,1152]{2,1,0:T(8,128)S(1)} %copy-done.1, s32[]{:T(128)S(6)} %select_n.29), kind=kOutput, calls=%fused_computation.6 | convolution fusion | flops 8155717632 | bytes 45416452 | tf_op jit(solution)/shard_map/orn,ofn->orf/dot_general | solution.py:57
  1057.8 280.2 %reduce-scatter.5.cloned.1.call-done = f32[72,8,1024]{2,1,0:T(8,128)} async-done(((f32[1152,8,1024]{2,1,0:T(8,128)}), f32[72,8,1024]{2,1,0:T(8,128)}) %reduce-scatter.5.cloned.1.call-update) | async-done | bytes 2359312 | tf_op jit(solution)/shard_map/reduce_scatter | solution.py:71
  1338.1 4.6 multiply_subtract_fusion
  (7 shorter events, 0.1 us)
Async XLA Ops:
  7.2 794.7 %copy-start = (f32[8,72,1152]{2,1,0:T(8,128)S(1)}, f32[8,72,1152]{2,1,0:T(8,128)}, u32[]{:S(2)}) copy-start(f32[8,72,1152]{2,1,0:T(8,128)} %param.14) | copy-start | bytes 7962628
  7.2 65.9 %reduce-scatter.3.cloned.1.call-start = ((), (), s32[]{:S(2)}) async-start(), calls=%async_computation.3 | async-start | bytes 7077888 | tf_op jit(solution)/shard_map/reduce_scatter | solution.py:50
  7.9 65.9 %copy-start.2 = (s32[4,4]{1,0:T(4,128)S(1)}, s32[4,4]{1,0:T(4,128)}, u32[]{:S(2)}) copy-start(s32[4,4]{1,0:T(4,128)} %param.11) | copy-start | bytes 196
  7.9 265.8 %all-gather.6.cloned.1.call-start = ((), (), s32[]{:S(2)}) async-start(), calls=%async_computation.6 | async-start | bytes 40108032 | tf_op jit(solution)/shard_map/all_gather | solution.py:51
  73.1 760.7 %all-gather.4.cloned.1.call-start = ((), (), s32[]{:S(2)}) async-start(), calls=%async_computation.4 | async-start | bytes 35651584 | tf_op jit(solution)/shard_map/all_gather | solution.py:54
  73.8 1264.3 %reduce-scatter.5.cloned.1.call-start = ((), (), s32[]{:S(2)}) async-start(), calls=%async_computation.5 | async-start | bytes 40108032 | tf_op jit(solution)/shard_map/reduce_scatter | solution.py:71
  971.1 43.9 %copy-start.1 = (f32[8,72,1152]{2,1,0:T(8,128)S(1)}, f32[8,72,1152]{2,1,0:T(8,128)}, u32[]{:S(2)}) copy-start(f32[8,72,1152]{2,1,0:T(8,128)} %param.12) | copy-start | bytes 7962628
Sparse Core Ops, SparseCore 0:
  10.3 62.6 reduce-scatter.2
  74.7 198.9 all-gather.5
  275.3 177.9 all-gather.3
  971.2 366.8 reduce-scatter.4
where the time goes:
time: 1360 us; the launch traced here: 1350 us
  waiting for transfers between devices  546 us (40%)
  blocking collectives  444 us (33%)
  matrix products  219 us (16%)
  local copies, waits for them, and re-layouts  91.8 us (7%)
  other arithmetic  34.8 us (3%)
  between operations  14.3 us (1%)
    all_to_all x1, blocking collectives, local(): lax.all_to_all(ordered, 'shard', split_axis=0, concat_axis=1, tiled=True)  444 us
    reduce_scatter x1, waiting for transfers between devices, local(): lax.psum_scatter(jnp.einsum('orf,ork->fok', left_basis, pulled, precision...  280 us
    all_gather x1, waiting for transfers between devices, local(): lax.all_gather(row_piece[None], ('tensor', 'section'), axis=0, tiled=True)  199 us
    reduce_scatter x1, waiting for transfers between devices, local(): lax.psum_scatter(local_part, 'shard', scatter_dimension=0, tiled=True)  65.1 us
    dot_general x1, matrix products, local(): jnp.einsum('ofc,ofn->ocn', grad_slab, full_grad, precision=exact_mode)  43.9 us
    dot_general x1, matrix products, local(): jnp.einsum('orn,ofn->orf', grad_band, full_grad, precision=exact_mode)  42.9 us
    dot_general x1, matrix products, local(): jnp.einsum('orn,onk->ork', turned, full_right, precision=exact_mode)  38.4 us
    transpose x1, local copies, waits for them, and re-layouts, local(): jnp.einsum('orf,ork->fok', left_basis, pulled, precision=exact_mode)  37.2 us
  transfers between devices with their start and end apart: 4, of which 3 were waited for; matrix products, arithmetic and copies ran while one was open for 15% of the time, Pallas kernels for 0%

commit v1 on v0

--- a/solution.py
+++ b/solution.py
@@ -78,29 +78,123 @@
     return (new_master, update_dir, new_left, new_right, new_moment_one, new_moment_two)
 
 
+def slotwise(
+    grad_parts,
+    master,
+    owner_map,
+    left_factor,
+    right_factor,
+    left_basis,
+    right_basis,
+    moment_one,
+    moment_two,
+):
+    mode = lax.Precision.HIGH
+    group = ("major", "section")
+    everyone = ("major", "minor", "section")
+    shards = lax.axis_size("shard")
+    majors = lax.axis_size("major")
+    sections = lax.axis_size("section")
+    members = 2 * majors * sections
+    slots = members // 2
+    side = lax.axis_index("minor")
+    _, source = slot_table(owner_map, shards)
+    height = left_basis.shape[2]
+    width = right_basis.shape[1]
+    rows = height // members
+    cols = width // members
+    part = width // shards
+
+    def swap(bands):
+        return lax.all_to_all(bands, group, split_axis=0, concat_axis=0, tiled=True)
+
+    def natural(gathered):
+        split = gathered.reshape((2, majors, sections) + gathered.shape[2:])
+        return jnp.swapaxes(split, 0, 1)
+
+    summed = lax.psum_scatter(grad_parts[0, 0, 0], "shard", scatter_dimension=1, tiled=True)
+    pieces = lax.all_to_all(
+        summed.reshape(members, rows, part), everyone, split_axis=0, concat_axis=0, tiled=True
+    )
+    ordered = jnp.take(pieces, source, axis=0)
+    mine = lax.all_to_all(ordered, "shard", split_axis=0, concat_axis=0, tiled=True)
+    mine = jnp.swapaxes(mine.reshape(shards, slots, rows, part), 0, 1)
+    bands = swap(mine)
+    whole = natural(lax.all_gather(bands, "minor", axis=0))
+    grad = jnp.swapaxes(whole, 3, 4).reshape(height, width)
+
+    left_half = swap(left_basis).reshape(height // 2, height)
+    left_full = lax.all_gather(left_half, "minor", axis=0)
+    right_half = swap(jnp.swapaxes(right_basis, 1, 2))
+    right_turned = natural(lax.all_gather(right_half, "minor", axis=0)).reshape(width, width)
+
+    turned = jnp.einsum("rf,fn->rn", left_half, grad, precision=mode)
+    rotated_half = jnp.einsum("rn,kn->rk", turned, right_turned, precision=mode)
+    rotated = swap(rotated_half.reshape(slots, rows, width))
+    new_moment_one = beta_one * moment_one + (1.0 - beta_one) * rotated
+    new_moment_two = beta_two * moment_two + (1.0 - beta_two) * rotated * rotated
+    first_fix = 1.0 - beta_one**step_count
+    second_fix = 1.0 - beta_two**step_count
+    scaled = new_moment_one / first_fix / (jnp.sqrt(new_moment_two / second_fix) + epsilon)
+    scaled_half = swap(scaled).reshape(height // 2, width)
+
+    band_rows = lax.dynamic_index_in_dim(
+        grad.reshape(majors, 2, sections * rows, width), side, 1, keepdims=False
+    ).reshape(height // 2, width)
+    left_product = jnp.einsum("rn,fn->rf", band_rows, grad, precision=mode)
+    band_cols = lax.dynamic_index_in_dim(
+        grad.reshape(height, majors, 2, sections * cols), side, 2, keepdims=False
+    ).reshape(height, width // 2)
+    right_product = jnp.einsum("fc,fn->cn", band_cols, grad, precision=mode)
+    new_left = beta_two * left_factor + (1.0 - beta_two) * swap(
+        left_product.reshape(slots, rows, height)
+    )
+    new_right = beta_two * right_factor + (1.0 - beta_two) * swap(
+        right_product.reshape(slots, cols, width)
+    )
+
+    pulled_half = jnp.einsum("rk,kn->rn", scaled_half, right_turned, precision=mode)
+    pulled = lax.all_gather(pulled_half, "minor", axis=0)
+    left_cols = lax.dynamic_index_in_dim(
+        left_full.reshape(height, majors, 2, sections * rows), side, 2, keepdims=False
+    ).reshape(height, height // 2)
+    update_half = jnp.einsum(
+        "rf,rn->fn", left_cols, pulled.reshape(height, width), precision=mode
+    )
+    update_dir = jnp.swapaxes(swap(update_half.reshape(slots, rows, width)), 0, 1)
+    new_master = master - learn_rate * (update_dir + decay_weight * master)
+    return (new_master, update_dir, new_left, new_right, new_moment_one, new_moment_two)
+
+
 def solution(mesh):
-    placed = (
-        P("shard", "tensor", "section", None, None),
-        P(("tensor", "section"), "shard", None),
-        P(),
-        P("shard", ("tensor", "section"), None),
-        P("shard", ("tensor", "section"), None),
-        P("shard", ("tensor", "section"), None),
-        P("shard", None, ("tensor", "section")),
-        P("shard", ("tensor", "section"), None),
-        P("shard", ("tensor", "section"), None),
-    )
-    return jax.shard_map(
-        local,
-        mesh=mesh,
-        in_specs=placed,
-        out_specs=(
-            P(("tensor", "section"), "shard", None),
-            P(("tensor", "section"), "shard", None),
-            P("shard", ("tensor", "section"), None),
-            P("shard", ("tensor", "section"), None),
-            P("shard", ("tensor", "section"), None),
-            P("shard", ("tensor", "section"), None),
-        ),
-        check_vma=False,
-    )
+    shards, tensors, sections = (mesh.shape[name] for name in ("shard", "tensor", "section"))
+
+    def run(*operands):
+        own = operands[3].shape[0] // shards
+        paired = tensors % 2 == 0 and 2 * own == tensors * sections
+        if paired:
+            shape = (shards, tensors // 2, 2, sections)
+            grid = jax.sharding.Mesh(
+                mesh.devices.reshape(shape), ("shard", "major", "minor", "section")
+            )
+            body, tensor = slotwise, ("major", "minor")
+        else:
+            grid, body, tensor = mesh, local, ("tensor",)
+        band = tensor + ("section",)
+        placed = (
+            P("shard", tensor, "section", None, None),
+            P(band, "shard", None),
+            P(),
+            P("shard", band, None),
+            P("shard", band, None),
+            P("shard", band, None),
+            P("shard", None, band),
+            P("shard", band, None),
+            P("shard", band, None),
+        )
+        results = (placed[1], placed[1], placed[3], placed[4], placed[7], placed[8])
+        return jax.shard_map(
+            body, mesh=grid, in_specs=placed, out_specs=results, check_vma=False
+        )(*operands)
+
+    return run

time: 1360 us -> 669 us (0.49)
  blocking collectives: 444 us -> 175 us
  waiting for transfers between devices: 546 us -> 286 us
  matrix products: 219 us -> 46.2 us
  starting transfers between devices: 0.15 us -> 28.6 us
  other arithmetic: 34.8 us -> 19.4 us
    reduce_scatter x2 -> x1, waiting for transfers between devices: 345 us -> 65.1 us  [slotwise(): lax.psum_scatter(grad_parts[0, 0, 0], 'shard', scatter_dimension=1, tiled...]
    all_to_all x1 -> x3, blocking collectives: 444 us -> 175 us  [the longest x2 114 us: swap(): return lax.all_to_all(bands, group, split_axis=0, concat_axis=0, tiled=True)]
    all_to_all x0 -> x7, waiting for transfers between devices: none -> 217 us  [the longest x6 191 us: swap(): return lax.all_to_all(bands, group, split_axis=0, concat_axis=0, tiled=True)]
    all_gather x2 -> x4, waiting for transfers between devices: 199 us -> 1.76 us  [the longest x1 1.7 us: slotwise(): whole = natural(lax.all_gather(bands, 'minor', axis=0))]
    dot_general x6, matrix products: 219 us -> 46.2 us  [the longest x1 9.36 us: slotwise(): jnp.einsum('rf,rn->fn', left_cols, pulled.reshape(height, width), precisi...]
    transpose x1, local copies, waits for them, and re-layouts: 37.2 us -> 0.24 us  [slotwise(): mine = jnp.swapaxes(mine.reshape(shards, slots, rows, part), 0, 1)]
    all_to_all x0 -> x7, starting transfers between devices: none -> 28.3 us  [the longest x6 24.5 us: swap(): return lax.all_to_all(bands, group, split_axis=0, concat_axis=0, tiled=True)]
    all_to_all x1 -> x0, local copies, waits for them, and re-layouts: 28 us -> none  [local(): lax.all_to_all(ordered, 'shard', split_axis=0, concat_axis=1, tiled=True)]
  transfers between devices with their start and end apart: 4 -> 12, of which waited for: 3 -> 9; matrix products, arithmetic and copies ran while one was open for 15% -> 19% of each run, Pallas kernels for 0% -> 0%
where the time goes in v1:
time: 669 us; the launch traced here: 660 us
  waiting for transfers between devices  286 us (43%)
  blocking collectives  175 us (26%)
  local copies, waits for them, and re-layouts  89.1 us (13%)
  matrix products  46.2 us (7%)
  starting transfers between devices  28.6 us (4%)
  other arithmetic  19.4 us (3%)
  between operations  16.1 us (2%)
    all_to_all x6, waiting for transfers between devices, swap(): return lax.all_to_all(bands, group, split_axis=0, concat_axis=0, tiled=True)  191 us
    all_to_all x2, blocking collectives, swap(): return lax.all_to_all(bands, group, split_axis=0, concat_axis=0, tiled=True)  114 us
    reduce_scatter x1, waiting for transfers between devices, slotwise(): lax.psum_scatter(grad_parts[0, 0, 0], 'shard', scatter_dimension=1, tiled...  65.1 us
    all_to_all x1, blocking collectives, slotwise(): lax.all_to_all(summed.reshape(members, rows, part), everyone, split_axis=...  60.7 us
    all_to_all x1, waiting for transfers between devices, slotwise(): lax.all_to_all(ordered, 'shard', split_axis=0, concat_axis=0, tiled=True)  26.2 us
    all_to_all x6, starting transfers between devices, swap(): return lax.all_to_all(bands, group, split_axis=0, concat_axis=0, tiled=True)  24.5 us
    unnamed x20, local copies, waits for them, and re-layouts  19.5 us
  transfers between devices with their start and end apart: 12, of which 9 were waited for; matrix products, arithmetic and copies ran while one was open for 19% of the time, Pallas kernels for 0%

profile of v1, /device:TPU:0, one launch (start us, length us, event | category | flops | bytes accessed | tf_op | source)
XLA Modules:
  0.0 659.9 jit_solution(14158763800405259468)
XLA Ops:
  8.7 65.1 %reduce-scatter.2.cloned.1.call-done = f32[1152,512]{1,0:T(8,128)} async-done(((f32[1152,1024]{1,0:T(8,128)}), f32[1152,512]{1,0:T(8,128)}) %reduce-scatter.2.cloned.1.call-update) | async-done | bytes 2359312 | tf_op jit(solution)/shard_map/reduce_scatter | solution.py:115
  73.9 60.7 %all_to_all.50 = f32[16,72,512]{2,1,0:T(8,128)S(1)} all-to-all(f32[16,72,512]{2,1,0:T(8,128)} %bitcast.74), channel_id=1, replica_groups=mesh['shard'=2,'major'=2,'minor'=2,'section'=4] {'major','minor','section'}, dimensions={0} | all-to-all | bytes 4718592 | tf_op jit(solution)/shard_map/all_to_all | solution.py:116
  134.6 4.5 all-to-all-start.4
  145.2 43.2 %all-to-all-done.4 = f32[8,64,1024]{2,1,0:T(8,128)} async-done(((f32[8,64,1024]{2,1,0:T(8,128)}), f32[8,64,1024]{2,1,0:T(8,128)}, u32[]{:S(2)}, u32[]{:S(2)}) %all-to-all-start.4) | async-done | bytes 2097184 | tf_op jit(solution)/shard_map/all_to_all | solution.py:109
  192.8 26.2 %all-to-all-done.2 = f32[16,72,512]{2,1,0:T(8,128)S(1)} async-done(((f32[16,72,512]{2,1,0:T(8,128)}), f32[16,72,512]{2,1,0:T(8,128)S(1)}, u32[]{:S(2)}, u32[]{:S(2)}) %all-to-all-start.2) | async-done | bytes 2359328 | tf_op jit(solution)/shard_map/all_to_all | solution.py:120
  219.2 57.2 %all_to_all.51 = f32[8,2,72,512]{3,2,1,0:T(8,128)} all-to-all(f32[8,2,72,512]{3,2,1,0:T(8,128)S(1)} %copy.74), channel_id=1, replica_groups=mesh['shard'=2,'major'=2,'minor'=2,'section'=4] {'major','section'}, dimensions={0} | all-to-all | bytes 4718592 | tf_op jit(solution)/shard_map/all_to_all | solution.py:109
  280.2 5.5 copy.76
  287.4 6.0 copy.75
  298.8 40.8 %all-to-all-done = f32[8,72,1152]{2,1,0:T(8,128)S(1)} async-done(((f32[8,72,1152]{2,1,0:T(8,128)}), f32[8,72,1152]{2,1,0:T(8,128)S(1)}, u32[]{:S(2)}, u32[]{:S(2)}) %all-to-all-start) | async-done | bytes 2654240 | tf_op jit(solution)/shard_map/all_to_all | solution.py:109
  339.6 8.0 %fusion.6 = f32[1024,576]{0,1:T(8,128)S(1)} fusion(f32[1152,1024]{1,0:T(8,128)} %bitcast.72, f32[576,1152]{1,0:T(8,128)S(1)} %bitcast.65), kind=kOutput, calls=%fused_computation.25 | convolution fusion | flops 4076863488 | bytes 9732096 | tf_op jit(solution)/shard_map/rf,fn->rn/dot_general | solution.py:131
  351.6 57.0 %all_to_all.52 = f32[8,72,1024]{2,1,0:T(8,128)S(1)} all-to-all(f32[8,72,1024]{2,1,0:T(8,128)S(1)} %fusion.7), channel_id=1, replica_groups=mesh['shard'=2,'major'=2,'minor'=2,'section'=4] {'major','section'}, dimensions={0} | all-to-all | bytes 4718592 | tf_op jit(solution)/shard_map/all_to_all | solution.py:109
  408.6 4.1 add_divide_fusion
  412.6 4.4 all-to-all-start.6
  417.6 7.6 %reshape.120 = f32[1152,1024,1]{1,0,2:T(8,128)} reshape(f32[2,2,4,72,2,512]{5,4,3,2,1,0:T(2,128)} %copy-done) | data formatting | bytes 9437184 | tf_op jit(solution)/shard_map/reshape | solution.py:124
  425.2 6.0 copy.80
  431.2 7.1 %reshape_reshape.7 = f32[1152,2,2,256]{3,2,0,1:T(2,128)} reshape(f32[2,2,4,72,2,512]{5,3,2,1,0,4:T(8,128)} %copy.80) | data formatting | bytes 9437184 | tf_op jit(solution)/shard_map/reshape;reshape | solution.py:146
  438.3 5.3 constant_dynamic-slice_fusion
  443.5 5.0 copy.81
  448.5 8.0 %fusion.10 = f32[8,64,1024]{2,1,0:T(8,128)} fusion(f32[8,64,1152]{2,1,0:T(8,128)S(1)} %bitcast.68, f32[1152,1024,1]{1,0,2:T(8,128)} %reshape.120), kind=kOutput, calls=%fused_computation.29 | convolution fusion | flops 3623878656 | bytes 9175040 | tf_op jit(solution)/shard_map/fc,fn->cn/dot_general | solution.py:148
  456.5 13.7 %all-to-all-done.6 = f32[8,72,1024]{2,1,0:T(8,128)} async-done(((f32[8,72,1024]{2,1,0:T(8,128)}), f32[8,72,1024]{2,1,0:T(8,128)}, u32[]{:S(2)}, u32[]{:S(2)}) %all-to-all-start.6) | async-done | bytes 2359328 | tf_op jit(solution)/shard_map/all_to_all | solution.py:109
  473.9 7.8 %reshape_reshape.6 = f32[2,2,288,1024]{3,2,1,0:T(8,128)} reshape(f32[2,2,4,72,2,512]{5,4,3,2,1,0:T(2,128)} %copy-done) | data formatting | bytes 9437184 | tf_op jit(solution)/shard_map/reshape;reshape | solution.py:142
  481.7 8.2 %fusion.8 = f32[576,1024]{1,0:T(8,128)} fusion(f32[576,1024]{1,0:T(8,128)} %bitcast.20, f32[1024,1024]{1,0:T(8,128)} %bitcast.60), kind=kOutput, calls=%fused_computation.27 | convolution fusion | flops 3623878656 | bytes 8912896 | tf_op jit(solution)/shard_map/rk,kn->rn/dot_general | solution.py:156
  491.8 8.7 %fusion.9 = f32[8,72,1152]{2,1,0:T(8,128)} fusion(f32[8,72,1024]{2,1,0:T(8,128)S(1)} %bitcast.70, f32[1152,1024,1]{1,0,2:T(8,128)} %reshape.120), kind=kOutput, calls=%fused_computation.28 | convolution fusion | flops 4076863488 | bytes 9732096 | tf_op jit(solution)/shard_map/rn,fn->rf/dot_general | solution.py:144
  500.5 20.9 %all-to-all-done.9 = f32[8,64,1024]{2,1,0:T(8,128)S(1)} async-done(((f32[8,64,1024]{2,1,0:T(8,128)}), f32[8,64,1024]{2,1,0:T(8,128)S(1)}, u32[]{:S(2)}, u32[]{:S(2)}) %all-to-all-start.9) | async-done | bytes 2097184 | tf_op jit(solution)/shard_map/all_to_all | solution.py:109
  522.7 4.6 all-to-all-start.8
  527.3 9.9 %reshape.121 = f32[1152,2,2,288]{3,2,1,0:T(2,128)} reshape(f32[2,576,1152]{2,1,0:T(8,128)} %all-gather.8.cloned.1.call-done) | data formatting | bytes 10616832 | tf_op jit(solution)/shard_map/reshape | solution.py:159
  537.3 5.1 constant_dynamic-slice_fusion.2
  542.4 7.2 %copy.85 = f32[1152,2,1,288]{0,3,2,1:T(8,128)} copy(f32[1152,2,1,288]{3,2,1,0:T(1,128)S(1)} %constant_dynamic-slice_fusion.2) | data formatting | bytes 5308416
  549.6 9.4 %fusion = f32[8,72,1024]{2,1,0:T(8,128)} fusion(f32[8,72,1152]{2,1,0:T(8,128)} %bitcast.67, f32[1152,1024]{1,0:T(8,128)} %all-gather.14.cloned.1.call-done), kind=kOutput, calls=%fused_computation.1 | convolution fusion | flops 4076863488 | bytes 9732096 | tf_op jit(solution)/shard_map/rf,rn->fn/dot_general | solution.py:161
  559.0 27.2 %all-to-all-done.8 = f32[8,72,1152]{2,1,0:T(8,128)} async-done(((f32[8,72,1152]{2,1,0:T(8,128)}), f32[8,72,1152]{2,1,0:T(8,128)}, u32[]{:S(2)}, u32[]{:S(2)}) %all-to-all-start.8) | async-done | bytes 2654240 | tf_op jit(solution)/shard_map/all_to_all | solution.py:109
  590.0 4.4 multiply_add_fusion.2
  598.0 45.1 %all-to-all-done.7 = f32[8,72,1024]{2,1,0:T(8,128)S(1)} async-done(((f32[8,72,1024]{2,1,0:T(8,128)}), f32[8,72,1024]{2,1,0:T(8,128)S(1)}, u32[]{:S(2)}, u32[]{:S(2)}) %all-to-all-start.7) | async-done | bytes 2359328 | tf_op jit(solution)/shard_map/all_to_all | solution.py:109
  (53 shorter events, 50.0 us)
Async XLA Ops:
  8.0 65.9 %reduce-scatter.2.cloned.1.call-start = ((), (), s32[]{:S(2)}) async-start(), calls=%async_computation.12 | async-start | bytes 7077888 | tf_op jit(solution)/shard_map/reduce_scatter | solution.py:115
  134.6 4.5 copy-start.7
  134.6 53.7 %all-to-all-start.4 = ((f32[8,64,1024]{2,1,0:T(8,128)}), f32[8,64,1024]{2,1,0:T(8,128)}, u32[]{:S(2)}, u32[]{:S(2)}) async-start(f32[8,64,1024]{2,1,0:T(8,128)} %bitcast.76), calls=%async_computation.5 | async-start | bytes 4194304 | tf_op jit(solution)/shard_map/all_to_all | solution.py:109
  188.3 30.7 %all-to-all-start.2 = ((f32[16,72,512]{2,1,0:T(8,128)}), f32[16,72,512]{2,1,0:T(8,128)S(1)}, u32[]{:S(2)}, u32[]{:S(2)}) async-start(f32[16,72,512]{2,1,0:T(8,128)} %broadcast_select_fusion), calls=%async_computation.3 | async-start | bytes 4718592 | tf_op jit(solution)/shard_map/all_to_all | solution.py:120
  192.1 88.0 %all-gather.12.cloned.1.call-start = ((), (), s32[]{:S(2)}) async-start(), calls=%async_computation.14 | async-start | bytes 6291456 | tf_op jit(solution)/shard_map/all_gather | solution.py:129
  192.7 94.6 %all-gather.10.cloned.1.call-start = ((), (), s32[]{:S(2)}) async-start(), calls=%async_computation.13 | async-start | bytes 7077888 | tf_op jit(solution)/shard_map/all_gather | solution.py:123
  276.5 63.1 %all-to-all-start = ((f32[8,72,1152]{2,1,0:T(8,128)}), f32[8,72,1152]{2,1,0:T(8,128)S(1)}, u32[]{:S(2)}, u32[]{:S(2)}) async-start(f32[8,72,1152]{2,1,0:T(8,128)} %param.14), calls=%async_computation | async-start | bytes 5308416 | tf_op jit(solution)/shard_map/all_to_all | solution.py:109
  293.3 2.2 copy-start
  339.6 8.1 %copy-start.2 = (f32[8,72,1152]{2,1,0:T(8,128)}, f32[8,72,1152]{2,1,0:T(8,128)S(1)}, u32[]{:S(2)}) copy-start(f32[8,72,1152]{2,1,0:T(8,128)S(1)} %all-to-all-done) | copy-start | bytes 7962628
  339.6 8.1 %copy-start.1 = (f32[2,2,4,64,1024]{4,3,2,0,1:T(8,128)S(1)}, f32[2,2,4,64,1024]{4,3,2,0,1:T(8,128)}, u32[]{:S(2)}) copy-start(f32[2,2,4,64,1024]{4,3,2,0,1:T(8,128)} %copy.76) | copy-start | bytes 12582916
  351.5 57.0 %copy-start.5 = (f32[8,72,1024]{2,1,0:T(8,128)S(1)}, f32[8,72,1024]{2,1,0:T(8,128)}, u32[]{:S(2)}) copy-start(f32[8,72,1024]{2,1,0:T(8,128)} %param.16) | copy-start | bytes 7077892
  351.6 57.0 %copy-start.6 = (f32[8,72,1024]{2,1,0:T(8,128)S(1)}, f32[8,72,1024]{2,1,0:T(8,128)}, u32[]{:S(2)}) copy-start(f32[8,72,1024]{2,1,0:T(8,128)} %param.17) | copy-start | bytes 7077892
  412.6 57.6 %all-to-all-start.6 = ((f32[8,72,1024]{2,1,0:T(8,128)}), f32[8,72,1024]{2,1,0:T(8,128)}, u32[]{:S(2)}, u32[]{:S(2)}) async-start(f32[8,72,1024]{2,1,0:T(8,128)} %get-tuple-element.48), calls=%async_computation.7 | async-start | bytes 4718592 | tf_op jit(solution)/shard_map/all_to_all | solution.py:109
  417.0 110.3 %all-gather.8.cloned.1.call-start = ((), (), s32[]{:S(2)}) async-start(), calls=%async_computation.11 | async-start | bytes 7962624 | tf_op jit(solution)/shard_map/all_gather | solution.py:127
  470.2 51.2 %all-to-all-start.9 = ((f32[8,64,1024]{2,1,0:T(8,128)}), f32[8,64,1024]{2,1,0:T(8,128)S(1)}, u32[]{:S(2)}, u32[]{:S(2)}) async-start(f32[8,64,1024]{2,1,0:T(8,128)} %fusion.10), calls=%async_computation.10 | async-start | bytes 4194304 | tf_op jit(solution)/shard_map/all_to_all | solution.py:109
  473.8 75.8 %all-gather.14.cloned.1.call-start = ((), (), s32[]{:S(2)}) async-start(), calls=%async_computation.15 | async-start | bytes 7077888 | tf_op jit(solution)/shard_map/all_gather | solution.py:157
  521.4 1.3 copy-start.3
  522.7 63.4 %all-to-all-start.8 = ((f32[8,72,1152]{2,1,0:T(8,128)}), f32[8,72,1152]{2,1,0:T(8,128)}, u32[]{:S(2)}, u32[]{:S(2)}) async-start(f32[8,72,1152]{2,1,0:T(8,128)} %fusion.9), calls=%async_computation.9 | async-start | bytes 5308416 | tf_op jit(solution)/shard_map/all_to_all | solution.py:109
  586.1 57.0 %all-to-all-start.7 = ((f32[8,72,1024]{2,1,0:T(8,128)}), f32[8,72,1024]{2,1,0:T(8,128)S(1)}, u32[]{:S(2)}, u32[]{:S(2)}) async-start(f32[8,72,1024]{2,1,0:T(8,128)} %fusion), calls=%async_computation.8 | async-start | bytes 4718592 | tf_op jit(solution)/shard_map/all_to_all | solution.py:109
  590.0 4.4 copy-start.4
Sparse Core Ops, SparseCore 0:
  11.1 62.6 reduce-scatter.1
Sparse Core Ops, SparseCore 1:
  194.1 11.4 all-gather.11
  276.5 10.8 all-gather.9
  419.7 15.6 all-gather.7
  490.1 14.7 all-gather.13

commit v2 on v1

--- a/solution.py
+++ b/solution.py
@@ -108,36 +108,44 @@
     def swap(bands):
         return lax.all_to_all(bands, group, split_axis=0, concat_axis=0, tiled=True)
 
-    def natural(gathered):
-        split = gathered.reshape((2, majors, sections) + gathered.shape[2:])
-        return jnp.swapaxes(split, 0, 1)
-
-    summed = lax.psum_scatter(grad_parts[0, 0, 0], "shard", scatter_dimension=1, tiled=True)
+    def across(axis, value):
+        return lax.ppermute(value, axis, [(0, 1), (1, 0)])
+
+    def in_order(index, own, other, axis):
+        lower = jnp.where(index == 0, own, other)
+        upper = jnp.where(index == 0, other, own)
+        return jnp.stack((lower, upper), axis=axis)
+
+    def natural(own, other):
+        shape = (majors, sections) + own.shape[1:]
+        return in_order(side, own.reshape(shape), other.reshape(shape), 1)
+
+    me = lax.axis_index("shard")
+    partial = grad_parts[0, 0, 0]
+    kept = lax.dynamic_slice_in_dim(partial, me * part, part, 1)
+    crossing = across("shard", lax.dynamic_slice_in_dim(partial, (1 - me) * part, part, 1))
+    left_half = swap(left_basis)
+    crossing, left_half = lax.optimization_barrier((crossing, left_half))
+    summed = kept + crossing
     pieces = lax.all_to_all(
         summed.reshape(members, rows, part), everyone, split_axis=0, concat_axis=0, tiled=True
     )
-    ordered = jnp.take(pieces, source, axis=0)
-    mine = lax.all_to_all(ordered, "shard", split_axis=0, concat_axis=0, tiled=True)
-    mine = jnp.swapaxes(mine.reshape(shards, slots, rows, part), 0, 1)
-    bands = swap(mine)
-    whole = natural(lax.all_gather(bands, "minor", axis=0))
+    right_bands = jnp.swapaxes(right_basis, 1, 2)
+    pieces, right_bands = lax.optimization_barrier((pieces, right_bands))
+    theirs = jnp.take(pieces, lax.dynamic_slice_in_dim(source, (1 - me) * slots, slots), axis=0)
+    ours = jnp.take(pieces, lax.dynamic_slice_in_dim(source, me * slots, slots), axis=0)
+    arrived = across("shard", theirs)
+    right_half = swap(right_bands)
+    arrived, right_half = lax.optimization_barrier((arrived, right_half))
+    bands = swap(in_order(me, ours, arrived, 1))
+    whole = natural(bands, across("minor", bands))
     grad = jnp.swapaxes(whole, 3, 4).reshape(height, width)
-
-    left_half = swap(left_basis).reshape(height // 2, height)
-    left_full = lax.all_gather(left_half, "minor", axis=0)
-    right_half = swap(jnp.swapaxes(right_basis, 1, 2))
-    right_turned = natural(lax.all_gather(right_half, "minor", axis=0)).reshape(width, width)
+    right_turned = natural(right_half, across("minor", right_half)).reshape(width, width)
+    left_other = across("minor", left_half).reshape(height // 2, height)
+    left_half = left_half.reshape(height // 2, height)
 
     turned = jnp.einsum("rf,fn->rn", left_half, grad, precision=mode)
     rotated_half = jnp.einsum("rn,kn->rk", turned, right_turned, precision=mode)
-    rotated = swap(rotated_half.reshape(slots, rows, width))
-    new_moment_one = beta_one * moment_one + (1.0 - beta_one) * rotated
-    new_moment_two = beta_two * moment_two + (1.0 - beta_two) * rotated * rotated
-    first_fix = 1.0 - beta_one**step_count
-    second_fix = 1.0 - beta_two**step_count
-    scaled = new_moment_one / first_fix / (jnp.sqrt(new_moment_two / second_fix) + epsilon)
-    scaled_half = swap(scaled).reshape(height // 2, width)
-
     band_rows = lax.dynamic_index_in_dim(
         grad.reshape(majors, 2, sections * rows, width), side, 1, keepdims=False
     ).reshape(height // 2, width)
@@ -146,6 +154,17 @@
         grad.reshape(height, majors, 2, sections * cols), side, 2, keepdims=False
     ).reshape(height, width // 2)
     right_product = jnp.einsum("fc,fn->cn", band_cols, grad, precision=mode)
+    rotated = swap(rotated_half.reshape(slots, rows, width))
+    rotated, left_product, right_product = lax.optimization_barrier(
+        (rotated, left_product, right_product)
+    )
+    new_moment_one = beta_one * moment_one + (1.0 - beta_one) * rotated
+    new_moment_two = beta_two * moment_two + (1.0 - beta_two) * rotated * rotated
+    first_fix = 1.0 - beta_one**step_count
+    second_fix = 1.0 - beta_two**step_count
+    scaled = new_moment_one / first_fix / (jnp.sqrt(new_moment_two / second_fix) + epsilon)
+    scaled_half = swap(scaled).reshape(height // 2, width)
+
     new_left = beta_two * left_factor + (1.0 - beta_two) * swap(
         left_product.reshape(slots, rows, height)
     )
@@ -154,13 +173,17 @@
     )
 
     pulled_half = jnp.einsum("rk,kn->rn", scaled_half, right_turned, precision=mode)
-    pulled = lax.all_gather(pulled_half, "minor", axis=0)
-    left_cols = lax.dynamic_index_in_dim(
-        left_full.reshape(height, majors, 2, sections * rows), side, 2, keepdims=False
-    ).reshape(height, height // 2)
+    pulled_other = across("minor", pulled_half)
+
+    def my_columns(half):
+        split = half.reshape(height // 2, majors, 2, sections * rows)
+        return lax.dynamic_index_in_dim(split, side, 2, keepdims=False).reshape(
+            height // 2, height // 2
+        )
+
     update_half = jnp.einsum(
-        "rf,rn->fn", left_cols, pulled.reshape(height, width), precision=mode
-    )
+        "rf,rn->fn", my_columns(left_half), pulled_half, precision=mode
+    ) + jnp.einsum("rf,rn->fn", my_columns(left_other), pulled_other, precision=mode)
     update_dir = jnp.swapaxes(swap(update_half.reshape(slots, rows, width)), 0, 1)
     new_master = master - learn_rate * (update_dir + decay_weight * master)
     return (new_master, update_dir, new_left, new_right, new_moment_one, new_moment_two)
@@ -171,7 +194,7 @@
 
     def run(*operands):
         own = operands[3].shape[0] // shards
-        paired = tensors % 2 == 0 and 2 * own == tensors * sections
+        paired = shards == 2 and tensors % 2 == 0 and 2 * own == tensors * sections
         if paired:
             shape = (shards, tensors // 2, 2, sections)
             grid = jax.sharding.Mesh(

time: 669 us -> 590 us (0.88)
  blocking collectives: 175 us -> 117 us
  waiting for transfers between devices: 286 us -> 254 us
  other arithmetic: 19.4 us -> 39.1 us
  between operations: 16.1 us -> 1.34 us
  starting transfers between devices: 28.6 us -> 37.1 us
    ppermute x0 -> x6, waiting for transfers between devices: none -> 74.2 us  [across(): return lax.ppermute(value, axis, [(0, 1), (1, 0)])]
    reduce_scatter x1 -> x0, waiting for transfers between devices: 65.1 us -> none  [slotwise(): lax.psum_scatter(grad_parts[0, 0, 0], 'shard', scatter_dimension=1, tiled...]
    all_to_all x2 -> x1, blocking collectives: 114 us -> 58.5 us  [swap(): return lax.all_to_all(bands, group, split_axis=0, concat_axis=0, tiled=True)]
    all_to_all x1 -> x0, waiting for transfers between devices: 26.2 us -> none  [slotwise(): lax.all_to_all(ordered, 'shard', split_axis=0, concat_axis=0, tiled=True)]
    reshape x2 -> x0, local copies, waits for them, and re-layouts: 15.4 us -> none  [the longest x1 9.9 us: slotwise(): left_full.reshape(height, majors, 2, sections * rows)]
    dynamic_slice x1 -> x5, local copies, waits for them, and re-layouts: 5.13 us -> 20.3 us  [the longest x4 17 us: my_columns(): lax.dynamic_index_in_dim(split, side, 2, keepdims=False)]
    all_to_all x6 -> x7, waiting for transfers between devices: 191 us -> 180 us  [swap(): return lax.all_to_all(bands, group, split_axis=0, concat_axis=0, tiled=True)]
    another operation x0 -> x4, other arithmetic: none -> 8.86 us  [in_order(): return jnp.stack((lower, upper), axis=axis)]
  transfers between devices with their start and end apart: 12 -> 13, of which waited for: 9 -> 9; matrix products, arithmetic and copies ran while one was open for 19% -> 22% of each run, Pallas kernels for 0% -> 0%
where the time goes in v2:
time: 590 us; the launch traced here: 585 us
  waiting for transfers between devices  254 us (43%)
  blocking collectives  117 us (20%)
  local copies, waits for them, and re-layouts  92.5 us (16%)
  matrix products  44.5 us (8%)
  other arithmetic  39.1 us (7%)
  starting transfers between devices  37.1 us (6%)
    all_to_all x7, waiting for transfers between devices, swap(): return lax.all_to_all(bands, group, split_axis=0, concat_axis=0, tiled=True)  180 us
    ppermute x6, waiting for transfers between devices, across(): return lax.ppermute(value, axis, [(0, 1), (1, 0)])  74.2 us
    all_to_all x1, blocking collectives, swap(): return lax.all_to_all(bands, group, split_axis=0, concat_axis=0, tiled=True)  58.5 us
    all_to_all x1, blocking collectives, slotwise(): lax.all_to_all(summed.reshape(members, rows, part), everyone, split_axis=...  58.4 us
    all_to_all x7, starting transfers between devices, swap(): return lax.all_to_all(bands, group, split_axis=0, concat_axis=0, tiled=True)  33.4 us
    dynamic_slice x4, local copies, waits for them, and re-layouts, my_columns(): lax.dynamic_index_in_dim(split, side, 2, keepdims=False)  17 us
    dynamic_slice x2, local copies, waits for them, and re-layouts, slotwise(): lax.dynamic_index_in_dim(grad.reshape(height, majors, 2, sections * cols)...  11.8 us
  transfers between devices with their start and end apart: 13, of which 9 were waited for; matrix products, arithmetic and copies ran while one was open for 22% of the time, Pallas kernels for 0%

profile of v2, /device:TPU:0, one launch (start us, length us, event | category | flops | bytes accessed | tf_op | source)
XLA Modules:
  0.0 585.1 jit_solution(10032697113946004202)
XLA Ops:
  0.6 7.3 %all-to-all-start = ((f32[8,72,1152]{2,1,0:T(8,128)}), f32[8,72,1152]{2,1,0:T(8,128)S(1)}, u32[]{:S(2)}, u32[]{:S(2)}) async-start(f32[8,72,1152]{2,1,0:T(8,128)} %param.16), calls=%async_computation | async-start | bytes 5308416 | tf_op jit(solution)/shard_map/all_to_all | solution.py:109
  12.7 51.5 %collective-permute-done = f32[1152,512]{1,0:T(8,128)} collective-permute-done((f32[1152,512]{1,0:T(8,128)}, f32[1152,512]{1,0:T(8,128)}, u32[]{:S(2)}, u32[]{:S(2)}) %collective-permute-start) | collective-permute-done | bytes 2359328 | tf_op jit(solution)/shard_map/ppermute | solution.py:112
  64.2 4.7 all-to-all-done
  71.9 58.4 %all_to_all.45 = f32[16,72,512]{2,1,0:T(8,128)} all-to-all(f32[16,72,512]{2,1,0:T(8,128)S(1)} %bitcast.71), channel_id=1, replica_groups=mesh['shard'=2,'major'=2,'minor'=2,'section'=4] {'major','minor','section'}, dimensions={0} | all-to-all | bytes 4718592 | tf_op jit(solution)/shard_map/all_to_all | solution.py:130
  146.0 22.7 %collective-permute-done.1 = f32[8,72,512]{2,1,0:T(8,128)} collective-permute-done((f32[8,72,512]{2,1,0:T(8,128)}, f32[8,72,512]{2,1,0:T(8,128)}, u32[]{:S(2)}, u32[]{:S(2)}) %collective-permute-start.1) | collective-permute-done | bytes 1179680 | tf_op jit(solution)/shard_map/ppermute | solution.py:112
  168.7 15.0 %all-to-all-done.2 = f32[8,64,1024]{2,1,0:T(8,128)} async-done(((f32[8,64,1024]{2,1,0:T(8,128)}), f32[8,64,1024]{2,1,0:T(8,128)}, u32[]{:S(2)}, u32[]{:S(2)}) %all-to-all-start.2) | async-done | bytes 2097184 | tf_op jit(solution)/shard_map/all_to_all | solution.py:109
  187.3 4.7 all-to-all-start.3
  192.1 53.5 %all-to-all-done.3 = f32[8,2,72,512]{3,2,1,0:T(8,128)} async-done(((f32[8,2,72,512]{3,2,1,0:T(8,128)}), f32[8,2,72,512]{3,2,1,0:T(8,128)}, u32[]{:S(2)}, u32[]{:S(2)}) %all-to-all-start.3) | async-done | bytes 2359328 | tf_op jit(solution)/shard_map/all_to_all | solution.py:109
  256.4 5.8 copy.51
  262.2 7.4 %reshape.187 = f32[1152,1024,1]{1,0,2:T(8,128)} reshape(f32[2,2,4,72,2,512]{5,4,3,2,1,0:T(2,128)} %copy.51) | data formatting | bytes 9437184 | tf_op jit(solution)/shard_map/reshape | solution.py:142
  269.6 7.7 %fusion.4 = f32[8,72,1024]{2,1,0:T(8,128)S(1)} fusion(f32[8,72,1152]{2,1,0:T(8,128)S(1)} %all-to-all-done, f32[1152,1024,1]{1,0,2:T(8,128)} %reshape.187), kind=kOutput, calls=%fused_computation.40 | convolution fusion | flops 4076863488 | bytes 9732096 | tf_op jit(solution)/shard_map/rf,fn->rn/dot_general | solution.py:147
  277.3 5.3 fusion.5
  287.0 7.4 %reshape_reshape.13 = f32[2,2,288,1024]{3,2,1,0:T(8,128)} reshape(f32[2,2,4,72,2,512]{5,4,3,2,1,0:T(2,128)} %copy.51) | data formatting | bytes 9437184 | tf_op jit(solution)/shard_map/reshape;reshape | solution.py:150
  294.4 5.2 copy.67
  299.5 6.8 %reshape_reshape.14 = f32[1152,2,2,256]{3,2,0,1:T(2,128)} reshape(f32[2,2,4,72,2,512]{5,3,2,1,0,4:T(8,128)} %bitcast.66) | data formatting | bytes 9437184 | tf_op jit(solution)/shard_map/reshape;reshape | solution.py:154
  306.3 5.3 constant_dynamic-slice_fusion
  311.6 6.5 %copy.55 = f32[1152,2,1,256]{0,3,1,2:T(8,128)} copy(f32[1152,2,1,256]{3,2,0,1:T(1,128)} %constant_dynamic-slice_fusion) | data formatting | bytes 4718592 | tf_op jit(solution)/shard_map/jit(dynamic_index_in_dim)/dynamic_slice | solution.py:153
  323.5 5.7 fusion.7
  329.1 6.4 %fusion.6 = f32[576,1152]{1,0:T(8,128)} fusion(f32[576,1024]{1,0:T(8,128)S(1)} %bitcast.76, f32[1152,1024]{1,0:T(8,128)S(1)} %bitcast.62), kind=kOutput, calls=%fused_computation.42 | convolution fusion | flops 4076863488 | bytes 9732096 | tf_op jit(solution)/shard_map/rn,fn->rf/dot_general | solution.py:152
  335.5 7.1 %all-to-all-done.4 = f32[8,72,1024]{2,1,0:T(8,128)} async-done(((f32[8,72,1024]{2,1,0:T(8,128)}), f32[8,72,1024]{2,1,0:T(8,128)}, u32[]{:S(2)}, u32[]{:S(2)}) %all-to-all-start.4) | async-done | bytes 2359328 | tf_op jit(solution)/shard_map/all_to_all | solution.py:109
  347.0 7.3 %add_divide_fusion = (f32[8,72,1024]{2,1,0:T(8,128)}, f32[8,72,1024]{2,1,0:T(8,128)}, f32[8,72,1024]{2,1,0:T(8,128)}) fusion(f32[8,72,1024]{2,1,0:T(8,128)} %all-to-all-done.4, f32[8,72,1024]{2,1,0:T(8,128)} %param.18, f32[8,72,1024]{2,1,0:T(8,128)} %param.19), kind=kLoop, calls=%fused_computation.12 | loop fusion | flops 5898240 | bytes 14155776 | tf_op jit(solution)/shard_map/div | solution.py:165
  354.3 41.9 %all-to-all-done.8 = f32[8,64,1024]{2,1,0:T(8,128)} async-done(((f32[8,64,1024]{2,1,0:T(8,128)}), f32[8,64,1024]{2,1,0:T(8,128)}, u32[]{:S(2)}, u32[]{:S(2)}) %all-to-all-start.8) | async-done | bytes 2097184 | tf_op jit(solution)/shard_map/all_to_all | solution.py:109
  396.3 58.5 %all_to_all.46 = f32[8,72,1024]{2,1,0:T(8,128)} all-to-all(f32[8,72,1024]{2,1,0:T(8,128)} %get-tuple-element.37), channel_id=1, replica_groups=mesh['shard'=2,'major'=2,'minor'=2,'section'=4] {'major','section'}, dimensions={0} | all-to-all | bytes 4718592 | tf_op jit(solution)/shard_map/all_to_all | solution.py:109
  454.7 4.6 all-to-all-start.7
  459.4 8.2 %fusion.8 = f32[576,1024]{1,0:T(8,128)} fusion(f32[576,1024]{1,0:T(8,128)} %bitcast.75, f32[1024,1024]{1,0:T(8,128)} %bitcast.63), kind=kOutput, calls=%fused_computation.44 | convolution fusion | flops 3623878656 | bytes 8912896 | tf_op jit(solution)/shard_map/rk,kn->rn/dot_general | solution.py:175
  472.6 4.7 constant_dynamic-slice_fusion.3
  477.3 4.9 copy.47
  482.2 5.9 %reshape_reshape.15 = f32[576,2,2,288]{3,2,1,0:T(2,128)} reshape(f32[8,72,1152]{2,1,0:T(8,128)} %collective-permute-done.4) | data formatting | bytes 5308416 | tf_op jit(solution)/shard_map/reshape;reshape | solution.py:179
  495.5 5.2 fusion.9
  500.7 6.0 %convolution_add_fusion = f32[576,1024]{1,0:T(8,128)} fusion(f32[576,1024]{1,0:T(8,128)S(1)} %fusion.9, f32[576,576]{0,1:T(8,128)S(1)} %bitcast.81, f32[576,1024]{1,0:T(8,128)} %collective-permute-done.5), kind=kOutput, calls=%fused_computation.15 | convolution fusion | flops 2039021568 | bytes 8404992 | tf_op jit(solution)/shard_map/rf,rn->fn/dot_general | solution.py:186
  506.7 12.2 %all-to-all-done.7 = f32[8,72,1152]{2,1,0:T(8,128)} async-done(((f32[8,72,1152]{2,1,0:T(8,128)}), f32[8,72,1152]{2,1,0:T(8,128)}, u32[]{:S(2)}, u32[]{:S(2)}) %all-to-all-start.7) | async-done | bytes 2654240 | tf_op jit(solution)/shard_map/all_to_all | solution.py:109
  530.6 45.1 %all-to-all-done.6 = f32[8,72,1024]{2,1,0:T(8,128)S(1)} async-done(((f32[8,72,1024]{2,1,0:T(8,128)}), f32[8,72,1024]{2,1,0:T(8,128)S(1)}, u32[]{:S(2)}, u32[]{:S(2)}) %all-to-all-start.6) | async-done | bytes 2359328 | tf_op jit(solution)/shard_map/all_to_all | solution.py:109
  (59 shorter events, 84.9 us)
Async XLA Ops:
  0.6 68.3 %all-to-all-start = ((f32[8,72,1152]{2,1,0:T(8,128)}), f32[8,72,1152]{2,1,0:T(8,128)S(1)}, u32[]{:S(2)}, u32[]{:S(2)}) async-start(f32[8,72,1152]{2,1,0:T(8,128)} %param.16), calls=%async_computation | async-start | bytes 5308416 | tf_op jit(solution)/shard_map/all_to_all | solution.py:109
  11.2 53.0 %collective-permute-start = (f32[1152,512]{1,0:T(8,128)}, f32[1152,512]{1,0:T(8,128)}, u32[]{:S(2)}, u32[]{:S(2)}) collective-permute-start(f32[1152,512]{1,0:T(8,128)} %dynamic-slice_bitcast_fusion), channel_id=1, source_target_pairs={{0,16},{16,0},{1,17},{17,1},{2,18},{18,2},{3,19},{19,3},{4,20},{20... | collective-permute-start | bytes 7077896 | tf_op jit(solution)/shard_map/ppermute | solution.py:112
  130.3 4.5 copy-start.4
  130.3 53.4 %all-to-all-start.2 = ((f32[8,64,1024]{2,1,0:T(8,128)}), f32[8,64,1024]{2,1,0:T(8,128)}, u32[]{:S(2)}, u32[]{:S(2)}) async-start(f32[8,64,1024]{2,1,0:T(8,128)} %bitcast.82), calls=%async_computation.2 | async-start | bytes 4194304 | tf_op jit(solution)/shard_map/all_to_all | solution.py:109
  141.1 27.5 %collective-permute-start.1 = (f32[8,72,512]{2,1,0:T(8,128)}, f32[8,72,512]{2,1,0:T(8,128)}, u32[]{:S(2)}, u32[]{:S(2)}) collective-permute-start(f32[8,72,512]{2,1,0:T(8,128)} %broadcast_select_fusion.4), channel_id=1, source_target_pairs={{0,16},{16,0},{1,17},{17,1},{2,18},{18,2},{3,19},{19,3},{4,20},{20... | collective-permute-start | bytes 3538952 | tf_op jit(solution)/shard_map/ppermute | solution.py:112
  187.3 58.2 %all-to-all-start.3 = ((f32[8,2,72,512]{3,2,1,0:T(8,128)}), f32[8,2,72,512]{3,2,1,0:T(8,128)}, u32[]{:S(2)}, u32[]{:S(2)}) async-start(f32[8,2,72,512]{3,2,1,0:T(8,128)} %pad_maximum_fusion.2), calls=%async_computation.3 | async-start | bytes 4718592 | tf_op jit(solution)/shard_map/all_to_all | solution.py:109
  192.0 53.6 %collective-permute-start.3 = (f32[8,64,1024]{2,1,0:T(8,128)}, f32[8,64,1024]{2,1,0:T(8,128)}, u32[]{:S(2)}, u32[]{:S(2)}) collective-permute-start(f32[8,64,1024]{2,1,0:T(8,128)} %all-to-all-done.2), channel_id=1, source_target_pairs={{0,4},{4,0},{1,5},{5,1},{2,6},{6,2},{3,7},{7,3},{8,12},{12,8},{9,1... | collective-permute-start | bytes 6291464 | tf_op jit(solution)/shard_map/ppermute | solution.py:112
  245.5 5.0 collective-permute-start.2
  269.6 7.7 %copy-start = (f32[2,2,4,64,1024]{4,3,2,1,0:T(8,128)S(1)}, f32[2,2,4,64,1024]{4,3,2,1,0:T(8,128)}, u32[]{:S(2)}) copy-start(f32[2,2,4,64,1024]{4,3,2,1,0:T(8,128)} %pad_maximum_fusion.1) | copy-start | bytes 12582916
  282.6 60.0 %all-to-all-start.4 = ((f32[8,72,1024]{2,1,0:T(8,128)}), f32[8,72,1024]{2,1,0:T(8,128)}, u32[]{:S(2)}, u32[]{:S(2)}) async-start(f32[8,72,1024]{2,1,0:T(8,128)} %fusion.5), calls=%async_computation.4 | async-start | bytes 4718592 | tf_op jit(solution)/shard_map/all_to_all | solution.py:109
  311.6 10.2 %slice-start = ((s8[4718592]{0:T(1024)(128)(4,1)}), s8[524288]{0:T(1024)(128)(4,1)S(1)}, s32[]{:S(2)}) async-start(s8[4718592]{0:T(1024)(128)(4,1)} %bitcast.67), calls=%async_computation.9 | async-start | bytes 1048576
  318.1 3.7 slice-start.1
  321.8 1.7 copy-start.1
  342.6 53.6 %all-to-all-start.8 = ((f32[8,64,1024]{2,1,0:T(8,128)}), f32[8,64,1024]{2,1,0:T(8,128)}, u32[]{:S(2)}, u32[]{:S(2)}) async-start(f32[8,64,1024]{2,1,0:T(8,128)} %bitcast.77), calls=%async_computation.8 | async-start | bytes 4194304 | tf_op jit(solution)/shard_map/all_to_all | solution.py:109
  454.7 64.2 %all-to-all-start.7 = ((f32[8,72,1152]{2,1,0:T(8,128)}), f32[8,72,1152]{2,1,0:T(8,128)}, u32[]{:S(2)}, u32[]{:S(2)}) async-start(f32[8,72,1152]{2,1,0:T(8,128)} %bitcast.69), calls=%async_computation.7 | async-start | bytes 5308416 | tf_op jit(solution)/shard_map/all_to_all | solution.py:109
  459.4 22.9 %collective-permute-start.4 = (f32[8,72,1152]{2,1,0:T(8,128)S(1)}, f32[8,72,1152]{2,1,0:T(8,128)}, u32[]{:S(2)}, u32[]{:S(2)}) collective-permute-start(f32[8,72,1152]{2,1,0:T(8,128)S(1)} %all-to-all-done), channel_id=1, source_target_pairs={{0,4},{4,0},{1,5},{5,1},{2,6},{6,2},{3,7},{7,3},{8,12},{12,8},{9,1... | collective-permute-start | bytes 7962632 | tf_op jit(solution)/shard_map/ppermute | solution.py:112
  467.7 33.0 %collective-permute-start.5 = (f32[576,1024]{1,0:T(8,128)}, f32[576,1024]{1,0:T(8,128)}, u32[]{:S(2)}, u32[]{:S(2)}) collective-permute-start(f32[576,1024]{1,0:T(8,128)} %fusion.8), channel_id=1, source_target_pairs={{0,4},{4,0},{1,5},{5,1},{2,6},{6,2},{3,7},{7,3},{8,12},{12,8},{9,1... | collective-permute-start | bytes 7077896 | tf_op jit(solution)/shard_map/ppermute | solution.py:112
  495.5 5.2 copy-start.2
  518.9 56.8 %all-to-all-start.6 = ((f32[8,72,1024]{2,1,0:T(8,128)}), f32[8,72,1024]{2,1,0:T(8,128)S(1)}, u32[]{:S(2)}, u32[]{:S(2)}) async-start(f32[8,72,1024]{2,1,0:T(8,128)} %bitcast.74), calls=%async_computation.6 | async-start | bytes 4718592 | tf_op jit(solution)/shard_map/all_to_all | solution.py:109
  522.5 4.4 copy-start.3
